TPU v7x, 32 devices: a whole 2x2x4 slice. The times are simulated.
32 devices in a mesh: fsdp: 16 (over z, y, core), tp: 2 (over x).
Axes of the slice: x: 2, y: 2, z: 4, core: 2. Of those that a mesh axis runs over, the one named last changes fastest.
Arguments:
- frames: bfloat16 [16, 1504, 1280], P('fsdp', 'tp'), may hold values from -6 to 6
- out_grad: bfloat16 [16, 1504, 1280], P('fsdp', 'tp'), may hold values from -6 to 6
- clip_lengths: int32 [16], replicated, may hold values from 1 to 1504, 18048 in all
- clip_order: int32 [16], replicated, may hold values from 0 to 15, each once
- w_query: bfloat16 [1280, 1280], P('fsdp', 'tp'), may hold values from -0.25 to 0.25
- w_key: bfloat16 [1280, 1280], P('fsdp', 'tp'), may hold values from -0.25 to 0.25
- w_value: bfloat16 [1280, 1280], P('fsdp', 'tp'), may hold values from -0.15625 to 0.15625
- b_query: bfloat16 [1280], P(('tp', 'fsdp')), may hold values from -3 to 3
- b_value: bfloat16 [1280], P(('tp', 'fsdp')), may hold values from -0.1796875 to 0.1796875
- w_out: bfloat16 [1280, 1280], P('tp', 'fsdp'), may hold values from -1.75 to 1.75
- b_out: bfloat16 [1280], P(('fsdp', 'tp')), may hold values from -3 to 3
- w_expand: bfloat16 [1280, 5120], P('fsdp', 'tp'), may hold values from -0.15625 to 0.15625
- b_expand: bfloat16 [5120], P(('tp', 'fsdp')), may hold values from -3 to 3
- w_reduce: bfloat16 [5120, 1280], P('tp', 'fsdp'), may hold values from -0.078125 to 0.078125
- b_reduce: bfloat16 [1280], P(('fsdp', 'tp')), may hold values from -3 to 3
- first_gain: bfloat16 [1280], P(('fsdp', 'tp')), may hold values from 0.099609375 to 1.8984375
- first_shift: bfloat16 [1280], P(('fsdp', 'tp')), may hold values from -2 to 2
- second_gain: bfloat16 [1280], P(('fsdp', 'tp')), may hold values from 0.099609375 to 1.8984375
- second_shift: bfloat16 [1280], P(('fsdp', 'tp')), may hold values from -2 to 2
Outputs:
- out_frames: bfloat16 [16, 1504, 1280], P('fsdp', 'tp')
- frames_grad: bfloat16 [16, 1504, 1280], P('fsdp', 'tp')
- w_query_grad: float32 [1280, 1280], P('fsdp', 'tp')
- w_key_grad: float32 [1280, 1280], P('fsdp', 'tp')
- w_value_grad: float32 [1280, 1280], P('fsdp', 'tp')
- b_query_grad: float32 [1280], P(('tp', 'fsdp'))
- b_value_grad: float32 [1280], P(('tp', 'fsdp'))
- w_out_grad: float32 [1280, 1280], P('tp', 'fsdp')
- b_out_grad: float32 [1280], P(('fsdp', 'tp'))
- w_expand_grad: float32 [1280, 5120], P('fsdp', 'tp')
- b_expand_grad: float32 [5120], P(('tp', 'fsdp'))
- w_reduce_grad: float32 [5120, 1280], P('tp', 'fsdp')
- b_reduce_grad: float32 [1280], P(('fsdp', 'tp'))
- first_gain_grad: float32 [1280], P(('fsdp', 'tp'))
- first_shift_grad: float32 [1280], P(('fsdp', 'tp'))
- second_gain_grad: float32 [1280], P(('fsdp', 'tp'))
- second_shift_grad: float32 [1280], P(('fsdp', 'tp'))
Inputs may be any that keep to these rules, and one draw needn't show every extreme that they name: `clip_lengths`: frames of each clip that keys may come from; they sum to 18048. `clip_order`: each clip stands in exactly one slot.
All inputs are finite; a program needn't handle non-finite values.
Results may differ from a plain program's by a relative error of at most 0.02.
Values may be sent and summed in bfloat16 or wider, within the bound.
No kernel may reach another device: no remote copies, remote signals or barrier semaphores. Data moves between devices by JAX's collectives and lax.ppermute only.
A program may use at most 448 MiB of HBM per device.

v0:
```python
import jax
import jax.numpy as jnp
from jax import lax
from jax.sharding import PartitionSpec as P

HD = 80
EPSILON = 1e-05
MASKED = -1000000000.0


def layer_norm(features, norm_gain, norm_shift):
    row_mean = jnp.mean(features, axis=-1, keepdims=True)
    centred = features - row_mean
    row_var = jnp.mean(centred * centred, axis=-1, keepdims=True)
    inverse = lax.rsqrt(row_var + EPSILON)
    normed = centred * inverse
    return (normed * norm_gain + norm_shift, normed, inverse)


def norm_back(upstream, normed, inverse, norm_gain):
    tilted = upstream * norm_gain
    return inverse * (
        tilted
        - jnp.mean(tilted, axis=-1, keepdims=True)
        - normed * jnp.mean(tilted * normed, axis=-1, keepdims=True)
    )


def gelu_exact(inputs):
    return jax.nn.gelu(inputs, approximate=False)


def masked_scores(queries, key_rows, length):
    scores = jnp.einsum("qhe,khe->hqk", queries, key_rows, preferred_element_type=jnp.float32)
    allowed = jnp.arange(scores.shape[-1]) < length
    return jnp.where(allowed[None, None, :], scores, MASKED)


def attend(inputs):
    queries, key_rows, value_rows, length = inputs
    scores = masked_scores(queries, key_rows, length)
    row_top = jnp.max(scores, axis=-1, keepdims=True)
    raised = jnp.exp(scores - row_top)
    row_sum = jnp.sum(raised, axis=-1, keepdims=True)
    weights = (raised / row_sum).astype(jnp.bfloat16)
    context = jnp.einsum("hqk,khe->qhe", weights, value_rows, preferred_element_type=jnp.float32)
    return (context.astype(jnp.bfloat16), row_top[..., 0] + jnp.log(row_sum[..., 0]))


def attend_back(inputs):
    queries, key_rows, value_rows, length, log_total, context_grad = inputs
    scores = masked_scores(queries, key_rows, length)
    probs = jnp.exp(scores - log_total[..., None])
    weights = probs.astype(jnp.bfloat16)
    value_grad = jnp.einsum(
        "hqk,qhe->khe", weights, context_grad, preferred_element_type=jnp.float32
    )
    weight_grad = jnp.einsum(
        "qhe,khe->hqk", context_grad, value_rows, preferred_element_type=jnp.float32
    )
    row_inner = jnp.sum(weight_grad * probs, axis=-1, keepdims=True)
    score_grad = (probs * (weight_grad - row_inner)).astype(jnp.bfloat16)
    query_grad = jnp.einsum(
        "hqk,khe->qhe", score_grad, key_rows, preferred_element_type=jnp.float32
    )
    key_grad = jnp.einsum("hqk,qhe->khe", score_grad, queries, preferred_element_type=jnp.float32)
    return (
        query_grad.astype(jnp.bfloat16),
        key_grad.astype(jnp.bfloat16),
        value_grad.astype(jnp.bfloat16),
    )


def gather_inward(w_query, w_key, w_value, b_query, b_value, w_expand, b_expand):
    return (
        lax.all_gather(w_query, "fsdp", axis=0, tiled=True),
        lax.all_gather(w_key, "fsdp", axis=0, tiled=True),
        lax.all_gather(w_value, "fsdp", axis=0, tiled=True),
        lax.all_gather(b_query, "fsdp", axis=0, tiled=True),
        lax.all_gather(b_value, "fsdp", axis=0, tiled=True),
        lax.all_gather(w_expand, "fsdp", axis=0, tiled=True),
        lax.all_gather(b_expand, "fsdp", axis=0, tiled=True),
    )


def gather_outward(w_out, w_reduce):
    return (
        lax.all_gather(w_out, "fsdp", axis=1, tiled=True),
        lax.all_gather(w_reduce, "fsdp", axis=1, tiled=True),
    )


def per_device(
    frames,
    out_grad,
    clip_lengths,
    clip_order,
    w_query,
    w_key,
    w_value,
    b_query,
    b_value,
    w_out,
    b_out,
    w_expand,
    b_expand,
    w_reduce,
    b_reduce,
    first_gain,
    first_shift,
    second_gain,
    second_shift,
):
    per_group = frames.shape[0]
    clip_count = clip_order.shape[0]
    slot_ids = lax.axis_index("fsdp") * per_group + jnp.arange(per_group, dtype=jnp.int32)
    every_clip = jnp.arange(clip_count, dtype=jnp.int32)
    clip_ids = jnp.sum(
        jnp.where(every_clip[None, :] == slot_ids[:, None], clip_order[None, :], 0), axis=1
    )
    lengths = jnp.sum(
        jnp.where(every_clip[None, :] == clip_ids[:, None], clip_lengths[None, :], 0), axis=1
    )
    norm_params = (
        lax.all_gather(first_gain, ("fsdp", "tp"), axis=0, tiled=True),
        lax.all_gather(first_shift, ("fsdp", "tp"), axis=0, tiled=True),
        lax.all_gather(second_gain, ("fsdp", "tp"), axis=0, tiled=True),
        lax.all_gather(second_shift, ("fsdp", "tp"), axis=0, tiled=True),
        lax.all_gather(b_out, ("fsdp", "tp"), axis=0, tiled=True),
        lax.all_gather(b_reduce, ("fsdp", "tp"), axis=0, tiled=True),
    )
    gain_one, shift_one, gain_two, shift_two, out_bias, reduce_bias = [
        tensor.astype(jnp.float32) for tensor in norm_params
    ]
    wq_all, wk_all, wv_all, bq_all, bv_all, we_all, be_all = gather_inward(
        w_query, w_key, w_value, b_query, b_value, w_expand, b_expand
    )
    wo_all, wr_all = gather_outward(w_out, w_reduce)
    q_factor = HD ** (-0.5)
    frames_wide = frames.astype(jnp.float32)
    norm_one, normed_one, inverse_one = layer_norm(frames_wide, gain_one, shift_one)
    first_rows = lax.all_gather(norm_one.astype(jnp.bfloat16), "tp", axis=1, tiled=True)
    seq_len = first_rows.shape[1]
    queries = (
        (
            jnp.einsum("csd,de->cse", first_rows, wq_all, preferred_element_type=jnp.float32)
            + bq_all.astype(jnp.float32)
        )
        * q_factor
    ).astype(jnp.bfloat16)
    keys = jnp.einsum("csd,de->cse", first_rows, wk_all, preferred_element_type=jnp.float32).astype(
        jnp.bfloat16
    )
    values = (
        jnp.einsum("csd,de->cse", first_rows, wv_all, preferred_element_type=jnp.float32)
        + bv_all.astype(jnp.float32)
    ).astype(jnp.bfloat16)
    head_shape = (per_group, seq_len, -1, HD)
    query_heads = queries.reshape(head_shape)
    key_heads = keys.reshape(head_shape)
    value_heads = values.reshape(head_shape)
    context, log_total = lax.map(attend, (query_heads, key_heads, value_heads, lengths))
    context_flat = context.reshape(per_group, seq_len, -1)
    attn_terms = jnp.einsum("cse,ed->csd", context_flat, wo_all, preferred_element_type=jnp.float32)
    attn_part = lax.psum_scatter(
        attn_terms.astype(jnp.bfloat16), "tp", scatter_dimension=1, tiled=True
    ).astype(jnp.float32)
    middle = frames_wide + attn_part + out_bias
    norm_two, normed_two, inverse_two = layer_norm(middle, gain_two, shift_two)
    second_rows = lax.all_gather(norm_two.astype(jnp.bfloat16), "tp", axis=1, tiled=True)
    expanded = jnp.einsum(
        "csd,df->csf", second_rows, we_all, preferred_element_type=jnp.float32
    ) + be_all.astype(jnp.float32)
    activated, gelu_pull = jax.vjp(gelu_exact, expanded)
    hidden = activated.astype(jnp.bfloat16)
    mlp_terms = jnp.einsum("csf,fd->csd", hidden, wr_all, preferred_element_type=jnp.float32)
    out_frames = (
        middle
        + lax.psum_scatter(
            mlp_terms.astype(jnp.bfloat16), "tp", scatter_dimension=1, tiled=True
        ).astype(jnp.float32)
        + reduce_bias
    ).astype(jnp.bfloat16)
    wq_all, wk_all, wv_all, bq_all, bv_all, we_all, be_all = gather_inward(
        w_query, w_key, w_value, b_query, b_value, w_expand, b_expand
    )
    wo_all, wr_all = gather_outward(w_out, w_reduce)
    grad_wide = out_grad.astype(jnp.float32)
    grad_rows = lax.all_gather(out_grad, "tp", axis=1, tiled=True)
    w_reduce_grad = jnp.einsum("csf,csd->fd", hidden, grad_rows, preferred_element_type=jnp.float32)
    hidden_grad = jnp.einsum("csd,fd->csf", grad_rows, wr_all, preferred_element_type=jnp.float32)
    expanded_grad = gelu_pull(hidden_grad)[0].astype(jnp.bfloat16)
    b_expand_grad = jnp.sum(expanded_grad.astype(jnp.float32), axis=(0, 1))
    w_expand_grad = jnp.einsum(
        "csd,csf->df", second_rows, expanded_grad, preferred_element_type=jnp.float32
    )
    second_terms = jnp.einsum(
        "csf,df->csd", expanded_grad, we_all, preferred_element_type=jnp.float32
    )
    second_grad = lax.psum_scatter(
        second_terms.astype(jnp.bfloat16), "tp", scatter_dimension=1, tiled=True
    ).astype(jnp.float32)
    second_gain_grad = jnp.sum(second_grad * normed_two, axis=(0, 1))
    second_shift_grad = jnp.sum(second_grad, axis=(0, 1))
    middle_grad = grad_wide + norm_back(second_grad, normed_two, inverse_two, gain_two)
    branch_grad = middle_grad.astype(jnp.bfloat16)
    b_out_grad = jnp.sum(branch_grad.astype(jnp.float32), axis=(0, 1))
    b_reduce_grad = jnp.sum(grad_wide, axis=(0, 1))
    branch_rows = lax.all_gather(branch_grad, "tp", axis=1, tiled=True)
    w_out_grad = jnp.einsum(
        "cse,csd->ed", context_flat, branch_rows, preferred_element_type=jnp.float32
    )
    context_grad = jnp.einsum(
        "csd,ed->cse", branch_rows, wo_all, preferred_element_type=jnp.float32
    ).astype(jnp.bfloat16)
    query_grad, key_grad, value_grad = lax.map(
        attend_back,
        (query_heads, key_heads, value_heads, lengths, log_total, context_grad.reshape(head_shape)),
    )
    query_grad = query_grad.reshape(per_group, seq_len, -1)
    key_grad = key_grad.reshape(per_group, seq_len, -1)
    value_grad = value_grad.reshape(per_group, seq_len, -1)
    w_query_grad = (
        jnp.einsum("csd,cse->de", first_rows, query_grad, preferred_element_type=jnp.float32)
        * q_factor
    )
    b_query_grad = jnp.sum(query_grad.astype(jnp.float32), axis=(0, 1)) * q_factor
    w_key_grad = jnp.einsum("csd,cse->de", first_rows, key_grad, preferred_element_type=jnp.float32)
    w_value_grad = jnp.einsum(
        "csd,cse->de", first_rows, value_grad, preferred_element_type=jnp.float32
    )
    b_value_grad = jnp.sum(value_grad.astype(jnp.float32), axis=(0, 1))
    first_terms = (
        jnp.einsum("cse,de->csd", query_grad, wq_all, preferred_element_type=jnp.float32) * q_factor
        + jnp.einsum("cse,de->csd", key_grad, wk_all, preferred_element_type=jnp.float32)
        + jnp.einsum("cse,de->csd", value_grad, wv_all, preferred_element_type=jnp.float32)
    )
    first_grad = lax.psum_scatter(
        first_terms.astype(jnp.bfloat16), "tp", scatter_dimension=1, tiled=True
    ).astype(jnp.float32)
    first_gain_grad = jnp.sum(first_grad * normed_one, axis=(0, 1))
    first_shift_grad = jnp.sum(first_grad, axis=(0, 1))
    frames_grad = (middle_grad + norm_back(first_grad, normed_one, inverse_one, gain_one)).astype(
        jnp.bfloat16
    )
    inward_grads = (
        lax.psum_scatter(
            w_query_grad.astype(jnp.bfloat16), "fsdp", scatter_dimension=0, tiled=True
        ).astype(jnp.float32),
        lax.psum_scatter(
            w_key_grad.astype(jnp.bfloat16), "fsdp", scatter_dimension=0, tiled=True
        ).astype(jnp.float32),
        lax.psum_scatter(
            w_value_grad.astype(jnp.bfloat16), "fsdp", scatter_dimension=0, tiled=True
        ).astype(jnp.float32),
        lax.psum_scatter(
            b_query_grad.astype(jnp.bfloat16), "fsdp", scatter_dimension=0, tiled=True
        ).astype(jnp.float32),
        lax.psum_scatter(
            b_value_grad.astype(jnp.bfloat16), "fsdp", scatter_dimension=0, tiled=True
        ).astype(jnp.float32),
        lax.psum_scatter(
            w_expand_grad.astype(jnp.bfloat16), "fsdp", scatter_dimension=0, tiled=True
        ).astype(jnp.float32),
        lax.psum_scatter(
            b_expand_grad.astype(jnp.bfloat16), "fsdp", scatter_dimension=0, tiled=True
        ).astype(jnp.float32),
    )
    outward_grads = (
        lax.psum_scatter(
            w_out_grad.astype(jnp.bfloat16), "fsdp", scatter_dimension=1, tiled=True
        ).astype(jnp.float32),
        lax.psum_scatter(
            w_reduce_grad.astype(jnp.bfloat16), "fsdp", scatter_dimension=1, tiled=True
        ).astype(jnp.float32),
    )
    small_grads = (
        lax.psum_scatter(first_gain_grad, ("fsdp", "tp"), scatter_dimension=0, tiled=True),
        lax.psum_scatter(first_shift_grad, ("fsdp", "tp"), scatter_dimension=0, tiled=True),
        lax.psum_scatter(second_gain_grad, ("fsdp", "tp"), scatter_dimension=0, tiled=True),
        lax.psum_scatter(second_shift_grad, ("fsdp", "tp"), scatter_dimension=0, tiled=True),
        lax.psum_scatter(b_out_grad, ("fsdp", "tp"), scatter_dimension=0, tiled=True),
        lax.psum_scatter(b_reduce_grad, ("fsdp", "tp"), scatter_dimension=0, tiled=True),
    )
    return (
        out_frames,
        frames_grad,
        inward_grads[0],
        inward_grads[1],
        inward_grads[2],
        inward_grads[3],
        inward_grads[4],
        outward_grads[0],
        small_grads[4],
        inward_grads[5],
        inward_grads[6],
        outward_grads[1],
        small_grads[5],
        small_grads[0],
        small_grads[1],
        small_grads[2],
        small_grads[3],
    )


def solution(mesh):
    return jax.shard_map(
        per_device,
        mesh=mesh,
        in_specs=(
            P("fsdp", "tp", None),
            P("fsdp", "tp", None),
            P(),
            P(),
            P("fsdp", "tp"),
            P("fsdp", "tp"),
            P("fsdp", "tp"),
            P(("tp", "fsdp")),
            P(("tp", "fsdp")),
            P("tp", "fsdp"),
            P(("fsdp", "tp")),
            P("fsdp", "tp"),
            P(("tp", "fsdp")),
            P("tp", "fsdp"),
            P(("fsdp", "tp")),
            P(("fsdp", "tp")),
            P(("fsdp", "tp")),
            P(("fsdp", "tp")),
            P(("fsdp", "tp")),
        ),
        out_specs=(
            P("fsdp", "tp", None),
            P("fsdp", "tp", None),
            P("fsdp", "tp"),
            P("fsdp", "tp"),
            P("fsdp", "tp"),
            P(("tp", "fsdp")),
            P(("tp", "fsdp")),
            P("tp", "fsdp"),
            P(("fsdp", "tp")),
            P("fsdp", "tp"),
            P(("tp", "fsdp")),
            P("tp", "fsdp"),
            P(("fsdp", "tp")),
            P(("fsdp", "tp")),
            P(("fsdp", "tp")),
            P(("fsdp", "tp")),
            P(("fsdp", "tp")),
        ),
        check_vma=False,
    )
```

profile of v0, /device:TPU:0, one launch (start us, length us, event | category | flops | bytes accessed | tf_op | source)
XLA Modules:
  0.0 1336.9 jit_solution(3240912666753867138)
XLA Ops:
  13.1 43.0 %all-reduce.19 = (bf16[1280]{0:T(1024)(128)(2,1)}, bf16[1280]{0:T(1024)(128)(2,1)}, bf16[1280]{0:T(1024)(128)(2,1)}, bf16[1280]{0:T(1024)(128)(2,1)S(1)}, bf16[1...) all-reduce(bf16[1280]{0:T(1024)(128)(2,1)S(1)} %dynamic-update-slice, ...), channel_id=1, replica_groups=mesh['fsdp'=16,'tp'=2] {'fsdp','tp'}, use_global_device_ids=true, to_apply=%add.6 | all-reduce | flops 7680 | bytes 30720
  56.1 1.9 convert_reduce_fusion.2
  58.0 2.2 fusion.35
  60.9 2.0 fusion.30
  70.1 60.0 %all-reduce.21 = (bf16[640]{0:T(1024)(128)(2,1)S(1)}, bf16[640]{0:T(1024)(128)(2,1)S(1)}, bf16[2560]{0:T(1024)(128)(2,1)}) all-reduce(bf16[640]{0:T(1024)(128)(2,1)S(1)} %dynamic-update-slice.2, bf16[640]{0:T(1024)(128)(2,1)S(1)} %dynamic-update-slice.3, ...), channel_id=1, replica_groups=mesh['fsdp'=16,'tp'=2] {'fsdp'}, use_global_device_ids=true, to_apply=%add.2 | all-reduce | flops 3840 | bytes 15360
  130.1 7.0 multiply_convert_fusion.2
  137.2 2.7 copy.57
  139.9 18.2 %all-gather.13.cloned.1.call-done = bf16[1280,640]{1,0:T(8,128)(2,1)} async-done(((bf16[80,640]{1,0:T(8,128)(2,1)}), bf16[1280,640]{1,0:T(8,128)(2,1)}) %all-gather.13.cloned.1.call-update) | async-done | bytes 1638416 | tf_op jit(solution)/shard_map/all_gather | solution.py:78
  158.1 7.0 add_convert_fusion.3
  165.1 4.0 copy.56
  169.1 29.9 %all-gather.17.cloned.1.call-done = bf16[1280,640]{1,0:T(8,128)(2,1)} async-done(((bf16[80,640]{1,0:T(8,128)(2,1)}), bf16[1280,640]{1,0:T(8,128)(2,1)}) %all-gather.17.cloned.1.call-update) | async-done | bytes 1638416 | tf_op jit(solution)/shard_map/all_gather | solution.py:77
  199.0 7.0 fusion.80
  206.0 4.0 copy.58
  210.0 28.8 %fusion.101 = (f32[8,1504]{1,0:T(8,128)S(1)}, f32[8,1504,1504]{1,2,0:T(8,128)}) fusion(bf16[1504,8,80]{0,2,1:T(8,128)(2,1)S(1)} %bitcast.117, bf16[1504,8,80]{0,2,1:T(8,128)(2,1)} %bitcast.119, pred[1504]{0:T(1024)(128)(4,1)S(1)} %iota_compare_fusion), kind=kOutput, calls=%fused_computation.138 | convolution fusion | flops 2931560704 | bytes 76284384 | tf_op jit(solution)/shard_map/while/body/eval_jaxpr/qhe,khe->hqk/dot_general | solution.py:34
  238.8 23.5 %fusion = f32[8,1504]{1,0:T(8,128)S(1)} fusion(f32[8,1504,1504]{1,2,0:T(8,128)} %get-tuple-element.104, f32[8,1504]{1,0:T(8,128)S(1)} %get-tuple-element.103), kind=kLoop, calls=%fused_computation.5 | loop fusion | flops 36180224 | bytes 72480768 | tf_op jit(solution)/shard_map/while/body/eval_jaxpr/reduce_sum | solution.py:44
  262.3 27.5 %fusion.95 = bf16[8,80,1504]{2,1,0:T(8,128)(2,1)} fusion(bf16[1504,8,80]{0,2,1:T(8,128)(2,1)S(1)} %bitcast.122, f32[8,1504,1504]{1,2,0:T(8,128)} %get-tuple-element.104, f32[8,1504]{1,0:T(8,128)S(1)} %fusion, f32[8,1504]{1,0:T(8,128)S(1)} %get-tuple-element.103), kind=kOutput, calls=%fused_computation.116 | convolution fusion | flops 2950631424 | bytes 76331008 | tf_op jit(solution)/shard_map/while/body/eval_jaxpr/hqk,khe->qhe/dot_general | solution.py:46
  289.8 7.1 fusion.17
  298.1 49.0 %reduce-scatter.11.cloned.1.call-done = bf16[1,752,1280]{2,1,0:T(8,128)(2,1)} async-done(((bf16[1,1504,1280]{2,1,0:T(8,128)(2,1)}), bf16[1,752,1280]{2,1,0:T(8,128)(2,1)}) %reduce-scatter.11.cloned.1.call-update) | async-done | bytes 1925136 | tf_op jit(solution)/shard_map/reduce_scatter | solution.py:165
  347.2 2.4 fusion.96
  351.2 2.3 add_convert_fusion.2
  354.9 58.2 %all-gather.23.cloned.1.call-done = bf16[1280,2560]{1,0:T(8,128)(2,1)} async-done(((bf16[80,2560]{1,0:T(8,128)(2,1)}), bf16[1280,2560]{1,0:T(8,128)(2,1)}) %all-gather.23.cloned.1.call-update) | async-done | bytes 6553616 | tf_op jit(solution)/shard_map/all_gather | solution.py:81
  413.1 53.7 %all-gather.21.cloned.1.call-done = bf16[1,1504,1280]{2,1,0:T(8,128)(2,1)} async-done(((bf16[1,752,1280]{2,1,0:T(8,128)(2,1)}), bf16[1,1504,1280]{2,1,0:T(8,128)(2,1)}) %all-gather.21.cloned.1.call-update) | async-done | bytes 3850256 | tf_op jit(solution)/shard_map/all_gather | solution.py:170
  466.8 46.3 %multiply_convert_fusion.1 = (bf16[1504,2560]{1,0:T(8,128)(2,1)}, f32[1504,2560]{1,0:T(8,128)}, f32[1504,2560]{1,0:T(8,128)}) fusion(f32[2560]{0:T(1024)S(1)} %convert_element_type.231, bf16[1280,2560]{1,0:T(8,128)(2,1)} %all-gather.23.cloned.1.call-done, bf16[1,1504,1280]{2,1,0:T(8,128)(2,1)} %all-gather.21.cloned.1.call-done), kind=kOutput, calls=%fused_computation.14 | convolution fusion | flops 10110730240 | bytes 48916480 | tf_op jit(solution)/shard_map/csd,df->csf/dot_general | solution.py:171
  513.1 8.2 all-gather.27.cloned.1.call-done
  521.3 65.8 %all-gather.25.cloned.1.call-done = bf16[2560,1280]{0,1:T(8,128)(2,1)} async-done(((bf16[2560,80]{0,1:T(8,128)(2,1)}), bf16[2560,1280]{0,1:T(8,128)(2,1)}) %all-gather.25.cloned.1.call-update) | async-done | bytes 6553616 | tf_op jit(solution)/shard_map/all_gather | solution.py:89
  587.1 27.5 %fusion.102 = (bf16[2560]{0:T(1024)(128)(2,1)}, bf16[1504,2560]{1,0:T(8,128)(2,1)}) fusion(f32[1504,2560]{1,0:T(8,128)} %get-tuple-element.98, bf16[2560,1280]{0,1:T(8,128)(2,1)} %all-gather.25.cloned.1.call-done, bf16[1,1504,1280]{2,1,0:T(8,128)(2,1)} %all-gather.27.cloned.1.call-done, f32[1504,2560]{1,0:T(8,128)} %get-tuple-element.105, ...), kind=kOutput, calls=%fused_computation.139 | convolution fusion | flops 9918216192 | bytes 48921600 | tf_op jit(solution)/shard_map/csd,fd->csf/dot_general | solution.py:191
  614.7 16.0 %fusion.16 = bf16[1,1504,1280]{2,1,0:T(8,128)(2,1)} fusion(bf16[1504,2560]{1,0:T(8,128)(2,1)} %get-tuple-element.113, bf16[1280,2560]{1,0:T(8,128)(2,1)} %all-gather.23.cloned.1.call-done), kind=kOutput, calls=%fused_computation.38 | convolution fusion | flops 9858539520 | bytes 18104320 | tf_op jit(solution)/shard_map/csf,df->csd/dot_general | solution.py:197
  630.7 15.6 %fusion.15 = bf16[1,1504,1280]{2,1,0:T(8,128)(2,1)} fusion(bf16[1504,2560]{1,0:T(8,128)(2,1)} %get-tuple-element.97, bf16[2560,1280]{0,1:T(8,128)(2,1)} %all-gather.25.cloned.1.call-done), kind=kOutput, calls=%fused_computation.37 | convolution fusion | flops 9858539520 | bytes 18104320 | tf_op jit(solution)/shard_map/csf,fd->csd/dot_general | solution.py:176
  647.0 33.4 %reduce-scatter.15.cloned.1.call-done = bf16[1,752,1280]{2,1,0:T(8,128)(2,1)} async-done(((bf16[1,1504,1280]{2,1,0:T(8,128)(2,1)}), bf16[1,752,1280]{2,1,0:T(8,128)(2,1)}) %reduce-scatter.15.cloned.1.call-update) | async-done | bytes 1925136 | tf_op jit(solution)/shard_map/reduce_scatter | solution.py:200
  680.5 4.8 fusion.41
  685.2 48.4 %reduce-scatter.13.cloned.1.call-done = bf16[1,752,1280]{2,1,0:T(8,128)(2,1)} async-done(((bf16[1,1504,1280]{2,1,0:T(8,128)(2,1)}), bf16[1,752,1280]{2,1,0:T(8,128)(2,1)}) %reduce-scatter.13.cloned.1.call-update) | async-done | bytes 1925136 | tf_op jit(solution)/shard_map/reduce_scatter | solution.py:179
  733.7 7.6 convert_reduce_fusion.5
  741.4 15.8 %convolution_convert_fusion = bf16[2560,1280]{0,1:T(8,128)(2,1)} fusion(bf16[1504,2560]{1,0:T(8,128)(2,1)} %get-tuple-element.97, bf16[1,1504,1280]{2,1,0:T(8,128)(2,1)} %all-gather.27.cloned.1.call-done), kind=kOutput, calls=%fused_computation.28 | convolution fusion | flops 9859891200 | bytes 18104320 | tf_op jit(solution)/shard_map/csf,csd->fd/dot_general | solution.py:190
  757.3 15.7 %convolution_convert_fusion.1 = bf16[1280,2560]{1,0:T(8,128)(2,1)} fusion(bf16[1504,2560]{1,0:T(8,128)(2,1)} %get-tuple-element.113, bf16[1,1504,1280]{2,1,0:T(8,128)(2,1)} %all-gather.21.cloned.1.call-done), kind=kOutput, calls=%fused_computation.29 | convolution fusion | flops 9859891200 | bytes 18104320 | tf_op jit(solution)/shard_map/csd,csf->df/dot_general | solution.py:194
  773.9 20.5 %all-gather.29.cloned.1.call-done = bf16[1,1504,1280]{2,1,0:T(8,128)(2,1)} async-done(((bf16[1,752,1280]{2,1,0:T(8,128)(2,1)}), bf16[1,1504,1280]{2,1,0:T(8,128)(2,1)}) %all-gather.29.cloned.1.call-update) | async-done | bytes 3850256 | tf_op jit(solution)/shard_map/all_gather | solution.py:209
  794.4 6.5 fusion.89
  800.9 2.7 copy.60
  803.6 7.3 fusion.92
  811.4 50.4 %multiply_reduce_fusion = (f32[8,1504]{1,0:T(8,128)S(1)}, f32[8,1504,1504]{1,2,0:T(8,128)}) fusion(f32[8,1504,1504]{1,2,0:T(8,128)} %get-tuple-element.104, f32[8,1504]{1,0:T(8,128)S(1)} %log_add_fusion, bf16[1504,8,80]{0,2,1:T(8,128)(2,1)S(1)} %bitcast.115, bf16[1504,8,80]{0,2,1:T(8,128)(2,1)} %bitcast.121), kind=kOutput, calls=%fused_computation.1 | convolution fusion | flops 2949656832 | bytes 148715520 | tf_op jit(solution)/shard_map/while/body/eval_jaxpr/qhe,khe->hqk/dot_general | solution.py:58
  861.8 27.5 %bitcast_reduce_fusion = (bf16[8,80]{1,0:T(8,128)(2,1)S(1)}, bf16[8,80,1504]{2,1,0:T(8,128)(2,1)}) fusion(bf16[1504,8,80]{0,2,1:T(8,128)(2,1)S(1)} %bitcast.116, f32[8,1504,1504]{1,2,0:T(8,128)} %get-tuple-element.104, f32[8,1504]{1,0:T(8,128)S(1)} %log_add_fusion), kind=kOutput, calls=%fused_computation.117 | convolution fusion | flops 2933497344 | bytes 76284160 | tf_op jit(solution)/shard_map/while/body/eval_jaxpr/hqk,qhe->khe/dot_general | solution.py:55
  889.3 7.3 fusion.86
  896.8 62.4 %multiply_convert_fusion = bf16[8,1504,1504]{1,2,0:T(8,128)(2,1)} fusion(f32[8,1504,1504]{1,2,0:T(8,128)} %get-tuple-element.107, f32[8,1504,1504]{1,2,0:T(8,128)} %get-tuple-element.104, f32[8,1504]{1,0:T(8,128)S(1)} %get-tuple-element.106, f32[8,1504]{1,0:T(8,128)S(1)} %log_add_fusion), kind=kLoop, calls=%fused_computation | loop fusion | flops 72384512 | bytes 181057536 | tf_op jit(solution)/shard_map/while/body/eval_jaxpr/convert_element_type | solution.py:62
  959.2 15.1 %convert_reduce_fusion.4 = (f32[8,80]{1,0:T(8,128)S(1)}, bf16[8,80,1504]{2,1,0:T(8,128)(2,1)S(1)}) fusion(bf16[1504,8,80]{0,2,1:T(8,128)(2,1)S(1)} %bitcast.120, bf16[8,1504,1504]{1,2,0:T(8,128)(2,1)} %multiply_convert_fusion), kind=kOutput, calls=%fused_computation.62 | convolution fusion | flops 2898267648 | bytes 40045056 | tf_op jit(solution)/shard_map/while/body/eval_jaxpr/hqk,khe->qhe/dot_general | solution.py:63
  974.3 1.3 copy-done.9
  975.6 6.7 fusion.77
  982.4 18.4 %convolution_convert_fusion.5 = bf16[8,80,1504]{2,1,0:T(8,128)(2,1)} fusion(bf16[1504,8,80]{0,2,1:T(8,128)(2,1)S(1)} %bitcast.118, bf16[8,1504,1504]{1,2,0:T(8,128)(2,1)} %multiply_convert_fusion), kind=kOutput, calls=%fused_computation.108 | convolution fusion | flops 2896343040 | bytes 40042496 | tf_op jit(solution)/shard_map/while/body/eval_jaxpr/hqk,qhe->khe/dot_general | solution.py:66
  1000.8 7.3 fusion.83
  1008.5 4.8 fusion.104
  1013.3 3.2 fusion.103
  1016.6 4.9 fusion.18
  1023.1 2.0 convert_element_type.275
  1025.0 2.0 convert_element_type.272
  1027.2 61.5 %all-reduce.20 = (bf16[640]{0:T(1024)(128)(2,1)S(1)}, bf16[640]{0:T(1024)(128)(2,1)S(1)}, bf16[2560]{0:T(1024)(128)(2,1)S(1)}) all-reduce(bf16[640]{0:T(1024)(128)(2,1)S(1)} %convert_element_type.265, bf16[640]{0:T(1024)(128)(2,1)S(1)} %reduce_sum.213, ...), channel_id=9, replica_groups=mesh['fsdp'=16,'tp'=2] {'fsdp'}, use_global_device_ids=true, to_apply=%region_21.22.clone | all-reduce | flops 3840 | bytes 15360
  1090.5 1.6 convert_element_type.269
  1092.1 8.4 reduce-scatter.23.cloned.1.call-done
  1100.5 1.6 convert_element_type.262
  1102.1 61.6 %reduce-scatter.19.cloned.1.call-done = bf16[80,640]{1,0:T(8,128)(2,1)} async-done(((bf16[1280,640]{1,0:T(8,128)(2,1)}), bf16[80,640]{1,0:T(8,128)(2,1)}) %reduce-scatter.19.cloned.1.call-update) | async-done | bytes 102416 | tf_op jit(solution)/shard_map/reduce_scatter | solution.py:247
  1163.7 1.6 convert_element_type.258
  1165.3 60.6 %reduce-scatter.21.cloned.1.call-done = bf16[80,640]{1,0:T(8,128)(2,1)} async-done(((bf16[1280,640]{1,0:T(8,128)(2,1)}), bf16[80,640]{1,0:T(8,128)(2,1)}) %reduce-scatter.21.cloned.1.call-update) | async-done | bytes 102416 | tf_op jit(solution)/shard_map/reduce_scatter | solution.py:250
  1225.9 1.6 convert_element_type.260
  1227.5 50.8 %reduce-scatter.17.cloned.1.call-done = bf16[1,752,1280]{2,1,0:T(8,128)(2,1)} async-done(((bf16[1,1504,1280]{2,1,0:T(8,128)(2,1)}), bf16[1,752,1280]{2,1,0:T(8,128)(2,1)}) %reduce-scatter.17.cloned.1.call-update) | async-done | bytes 1925136 | tf_op jit(solution)/shard_map/reduce_scatter | solution.py:238
  1278.4 3.4 fusion.42
  1281.8 40.1 %all-reduce.18 = (f32[1280]{0:T(1024)S(1)}, f32[1280]{0:T(1024)S(1)}, f32[1280]{0:T(1024)S(1)}, f32[1280]{0:T(1024)S(1)}, f32[1280]{0:T(1024)S(1)}, /*index=5*/f32[1280]{0:T(1024)S(1)}) all-reduce(f32[1280]{0:T(1024)S(1)} %copy-done.32, f32[1280]{0:T(1024)S(1)} %copy-done.33, ...), channel_id=12, replica_groups=mesh['fsdp'=16,'tp'=2] {'fsdp','tp'}, use_global_device_ids=true, to_apply=%region_26.27.clone | all-reduce | flops 7680 | bytes 61440
  1325.5 4.3 fusion.34
  (197 shorter events, 24.6 us)
Async XLA Ops:
  7.2 53.7 %copy-start = (bf16[1,752,1280]{2,1,0:T(8,128)(2,1)S(1)}, bf16[1,752,1280]{2,1,0:T(8,128)(2,1)}, u32[]{:S(2)}) copy-start(bf16[1,752,1280]{2,1,0:T(8,128)(2,1)} %param.19) | copy-start | bytes 5775364
  7.2 122.9 %all-gather.15.cloned.1.call-start = ((), (), s32[]{:S(2)}) async-start(), calls=%async_computation.12 | async-start | bytes 1740800 | tf_op jit(solution)/shard_map/all_gather | solution.py:76
  7.9 122.2 %all-gather.11.cloned.1.call-start = ((), (), s32[]{:S(2)}) async-start(), calls=%async_computation.10 | async-start | bytes 5775360 | tf_op jit(solution)/shard_map/all_gather | solution.py:142
  56.1 4.2 copy-start.22
  57.9 2.3 copy-start.24
  58.0 6.9 copy-start.42
  58.0 8.8 copy-start.45
  58.0 9.4 copy-start.46
  58.0 11.4 copy-start.47
  58.0 11.6 copy-start.48
  58.0 11.8 copy-start.49
  62.9 95.2 %all-gather.13.cloned.1.call-start = ((), (), s32[]{:S(2)}) async-start(), calls=%async_computation.11 | async-start | bytes 1740800 | tf_op jit(solution)/shard_map/all_gather | solution.py:78
  63.6 135.3 %all-gather.17.cloned.1.call-start = ((), (), s32[]{:S(2)}) async-start(), calls=%async_computation.13 | async-start | bytes 1740800 | tf_op jit(solution)/shard_map/all_gather | solution.py:77
  64.2 225.6 %all-gather.19.cloned.1.call-start = ((), (), s32[]{:S(2)}) async-start(), calls=%async_computation.14 | async-start | bytes 1740800 | tf_op jit(solution)/shard_map/all_gather | solution.py:88
  64.8 282.3 %reduce-scatter.11.cloned.1.call-start = ((), (), s32[]{:S(2)}) async-start(), calls=%async_computation.15 | async-start | bytes 5775360 | tf_op jit(solution)/shard_map/reduce_scatter | solution.py:165
  139.9 70.1 %copy-start.5 = (bf16[1504,640]{0,1:T(8,128)(2,1)}, bf16[1504,640]{0,1:T(8,128)(2,1)S(1)}, u32[]{:S(2)}) copy-start(bf16[1504,640]{0,1:T(8,128)(2,1)S(1)} %copy.57) | copy-start | bytes 5775364
  238.8 23.5 %copy-start.14 = (f32[8,1504]{1,0:T(8,128)}, f32[8,1504]{1,0:T(8,128)S(1)}, u32[]{:S(2)}) copy-start(f32[8,1504]{1,0:T(8,128)S(1)} %get-tuple-element.103) | copy-start | bytes 144388
  238.8 23.5 %copy-start.8 = (bf16[1504,640]{0,1:T(8,128)(2,1)S(1)}, bf16[1504,640]{0,1:T(8,128)(2,1)}, u32[]{:S(2)}) copy-start(bf16[1504,640]{0,1:T(8,128)(2,1)} %copy.56) | copy-start | bytes 5775364
  262.3 27.5 %copy-start.18 = (f32[8,1504]{1,0:T(8,128)}, f32[8,1504]{1,0:T(8,128)S(1)}, u32[]{:S(2)}) copy-start(f32[8,1504]{1,0:T(8,128)S(1)} %fusion) | copy-start | bytes 144388
  297.0 1.1 copy-start.41
  297.0 1.1 copy-start.40
  297.0 1.1 copy-start.39
  297.0 50.2 %copy-start.1 = (bf16[1,752,1280]{2,1,0:T(8,128)(2,1)S(1)}, bf16[1,752,1280]{2,1,0:T(8,128)(2,1)}, u32[]{:S(2)}) copy-start(bf16[1,752,1280]{2,1,0:T(8,128)(2,1)} %param.19) | copy-start | bytes 5775364
  297.0 116.1 %all-gather.23.cloned.1.call-start = ((), (), s32[]{:S(2)}) async-start(), calls=%async_computation.17 | async-start | bytes 6963200 | tf_op jit(solution)/shard_map/all_gather | solution.py:81
  297.8 169.0 %all-gather.21.cloned.1.call-start = ((), (), s32[]{:S(2)}) async-start(), calls=%async_computation.16 | async-start | bytes 5775360 | tf_op jit(solution)/shard_map/all_gather | solution.py:170
  298.1 52.5 %copy-start.16 = (f32[1280]{0:T(1024)}, f32[1280]{0:T(1024)S(1)}, u32[]{:S(2)}) copy-start(f32[1280]{0:T(1024)S(1)} %convert_element_type.227) | copy-start | bytes 15364
  298.1 52.4 %copy-start.20 = (f32[1280]{0:T(1024)}, f32[1280]{0:T(1024)S(1)}, u32[]{:S(2)}) copy-start(f32[1280]{0:T(1024)S(1)} %convert_element_type.228) | copy-start | bytes 15364
  347.2 2.4 copy-start.4
  351.2 3.7 copy-start.37
  353.5 167.8 %all-gather.27.cloned.1.call-start = ((), (), s32[]{:S(2)}) async-start(), calls=%async_computation.20 | async-start | bytes 5775360 | tf_op jit(solution)/shard_map/all_gather | solution.py:189
  354.3 232.9 %all-gather.25.cloned.1.call-start = ((), (), s32[]{:S(2)}) async-start(), calls=%async_computation.18 | async-start | bytes 6963200 | tf_op jit(solution)/shard_map/all_gather | solution.py:89
  354.9 325.6 %reduce-scatter.15.cloned.1.call-start = ((), (), s32[]{:S(2)}) async-start(), calls=%async_computation.21 | async-start | bytes 5775360 | tf_op jit(solution)/shard_map/reduce_scatter | solution.py:200
  630.7 103.0 %reduce-scatter.13.cloned.1.call-start = ((), (), s32[]{:S(2)}) async-start(), calls=%async_computation.19 | async-start | bytes 5775360 | tf_op jit(solution)/shard_map/reduce_scatter | solution.py:179
  646.3 34.1 %copy-start.2 = (bf16[1,752,1280]{2,1,0:T(8,128)(2,1)S(1)}, bf16[1,752,1280]{2,1,0:T(8,128)(2,1)}, u32[]{:S(2)}) copy-start(bf16[1,752,1280]{2,1,0:T(8,128)(2,1)} %param.19) | copy-start | bytes 5775364
  646.3 34.1 %copy-start.17 = (f32[1280]{0:T(1024)S(1)}, f32[1280]{0:T(1024)}, u32[]{:S(2)}) copy-start(f32[1280]{0:T(1024)} %copy-done.16) | copy-start | bytes 15364
  646.3 34.1 %copy-start.21 = (f32[1280]{0:T(1024)S(1)}, f32[1280]{0:T(1024)}, u32[]{:S(2)}) copy-start(f32[1280]{0:T(1024)} %copy-done.20) | copy-start | bytes 15364
  646.4 34.1 %copy-start.27 = (f32[752]{0:T(1024)S(1)}, f32[752]{0:T(1024)}, u32[]{:S(2)}) copy-start(f32[752]{0:T(1024)} %copy-done.26) | copy-start | bytes 9028
  646.4 34.1 %copy-start.31 = (f32[752]{0:T(1024)S(1)}, f32[752]{0:T(1024)}, u32[]{:S(2)}) copy-start(f32[752]{0:T(1024)} %copy-done.30) | copy-start | bytes 9028
  646.4 148.0 %all-gather.29.cloned.1.call-start = ((), (), s32[]{:S(2)}) async-start(), calls=%async_computation.22 | async-start | bytes 5775360 | tf_op jit(solution)/shard_map/all_gather | solution.py:209
  741.3 281.7 %reduce-scatter.29.cloned.1.call-start = ((), (), s32[]{:S(2)}) async-start(), calls=%async_computation.29 | async-start | bytes 6963200 | tf_op jit(solution)/shard_map/reduce_scatter | solution.py:273
  757.2 267.8 %reduce-scatter.27.cloned.1.call-start = ((), (), s32[]{:S(2)}) async-start(), calls=%async_computation.28 | async-start | bytes 6963200 | tf_op jit(solution)/shard_map/reduce_scatter | solution.py:262
  773.0 21.3 %copy-start.44 = (bf16[640,1280]{0,1:T(8,128)(2,1)S(1)}, bf16[640,1280]{0,1:T(8,128)(2,1)}, u32[]{:S(2)}) copy-start(bf16[640,1280]{0,1:T(8,128)(2,1)} %all-gather.19.cloned.1.call-done) | copy-start | bytes 4915204
  773.1 317.4 %reduce-scatter.25.cloned.1.call-start = ((), (), s32[]{:S(2)}) async-start(), calls=%async_computation.27 | async-start | bytes 1740800 | tf_op jit(solution)/shard_map/reduce_scatter | solution.py:270
  810.9 289.6 %reduce-scatter.23.cloned.1.call-start = ((), (), s32[]{:S(2)}) async-start(), calls=%async_computation.26 | async-start | bytes 1740800 | tf_op jit(solution)/shard_map/reduce_scatter | solution.py:253
  896.6 267.1 %reduce-scatter.19.cloned.1.call-start = ((), (), s32[]{:S(2)}) async-start(), calls=%async_computation.24 | async-start | bytes 1740800 | tf_op jit(solution)/shard_map/reduce_scatter | solution.py:247
  896.8 62.4 %copy-start.7 = (bf16[1504,640]{0,1:T(8,128)(2,1)S(1)}, bf16[1504,640]{0,1:T(8,128)(2,1)}, u32[]{:S(2)}) copy-start(bf16[1504,640]{0,1:T(8,128)(2,1)} %copy.58) | copy-start | bytes 5775364
  974.3 1.3 copy-start.9
  975.6 6.8 copy-start.6
  982.3 243.6 %reduce-scatter.21.cloned.1.call-start = ((), (), s32[]{:S(2)}) async-start(), calls=%async_computation.25 | async-start | bytes 1740800 | tf_op jit(solution)/shard_map/reduce_scatter | solution.py:250
  1000.8 7.6 copy-start.11
  1008.2 270.2 %reduce-scatter.17.cloned.1.call-start = ((), (), s32[]{:S(2)}) async-start(), calls=%async_computation.23 | async-start | bytes 5775360 | tf_op jit(solution)/shard_map/reduce_scatter | solution.py:238
  1008.4 4.9 copy-start.12
  1008.5 4.9 copy-start.43
  1013.3 3.2 copy-start.10
  1013.3 3.2 copy-start.13
  1021.5 5.7 copy-start.36
  1021.5 256.8 %copy-start.3 = (bf16[1,752,1280]{2,1,0:T(8,128)(2,1)S(1)}, bf16[1,752,1280]{2,1,0:T(8,128)(2,1)}, u32[]{:S(2)}) copy-start(bf16[1,752,1280]{2,1,0:T(8,128)(2,1)} %param.19) | copy-start | bytes 5775364
  1021.5 256.8 %copy-start.23 = (f32[1280]{0:T(1024)S(1)}, f32[1280]{0:T(1024)}, u32[]{:S(2)}) copy-start(f32[1280]{0:T(1024)} %copy-done.22) | copy-start | bytes 15364
  1021.5 256.8 %copy-start.25 = (f32[752]{0:T(1024)S(1)}, f32[752]{0:T(1024)}, u32[]{:S(2)}) copy-start(f32[752]{0:T(1024)} %copy-done.24) | copy-start | bytes 9028
  1021.5 256.8 %copy-start.29 = (f32[752]{0:T(1024)S(1)}, f32[752]{0:T(1024)}, u32[]{:S(2)}) copy-start(f32[752]{0:T(1024)} %copy-done.28) | copy-start | bytes 9028
  1021.6 260.2 %copy-start.32 = (f32[1280]{0:T(1024)S(1)}, f32[1280]{0:T(1024)}, u32[]{:S(2)}) copy-start(f32[1280]{0:T(1024)} %get-tuple-element.94) | copy-start | bytes 15364
  1021.6 260.2 %copy-start.33 = (f32[1280]{0:T(1024)S(1)}, f32[1280]{0:T(1024)}, u32[]{:S(2)}) copy-start(f32[1280]{0:T(1024)} %get-tuple-element.100) | copy-start | bytes 15364
  1021.6 260.2 %copy-start.34 = (f32[1280]{0:T(1024)S(1)}, f32[1280]{0:T(1024)}, u32[]{:S(2)}) copy-start(f32[1280]{0:T(1024)} %get-tuple-element.68) | copy-start | bytes 15364
  1021.6 260.2 %copy-start.35 = (f32[1280]{0:T(1024)S(1)}, f32[1280]{0:T(1024)}, u32[]{:S(2)}) copy-start(f32[1280]{0:T(1024)} %get-tuple-element.74) | copy-start | bytes 15364
  (6 other events, 4.5 us)
Sparse Core Ops, SparseCore 0:
  10.2 42.8 all-gather.14
  63.0 52.8 all-gather.10
  118.1 39.9 all-gather.12
  160.1 38.8 all-gather.16
  201.0 38.8 all-gather.18
  297.1 49.9 reduce-scatter.10
  349.7 63.3 all-gather.22
  415.3 51.4 all-gather.20
  468.4 52.8 all-gather.26
  523.7 63.3 all-gather.24
  630.8 49.6 reduce-scatter.14
  682.5 51.0 reduce-scatter.12
  741.5 52.8 all-gather.28
  798.7 86.9 reduce-scatter.28
  889.5 85.9 reduce-scatter.26
  979.6 58.4 reduce-scatter.24
  1041.6 58.8 reduce-scatter.22
  1105.1 58.5 reduce-scatter.18
  1167.4 58.4 reduce-scatter.20
  1228.1 50.1 reduce-scatter.16
where the time goes:
time: 1340 us
  waiting for transfers between devices  571 us (43%)
  matrix products  381 us (28%)
  blocking collectives  205 us (15%)
  other arithmetic  133 us (10%)
  local copies, waits for them, and re-layouts  27.2 us (2%)
  between operations  18 us (1%)
    unnamed x4, blocking collectives  205 us
    all_gather x1, waiting for transfers between devices, gather_outward(): lax.all_gather(w_reduce, 'fsdp', axis=1, tiled=True)  65.8 us
    convert_element_type x1, other arithmetic, attend_back(): score_grad = (probs * (weight_grad - row_inner)).astype(jnp.bfloat16)  62.4 us
    reduce_scatter x1, waiting for transfers between devices, per_device(): lax.psum_scatter(w_query_grad.astype(jnp.bfloat16), 'fsdp', scatter_dimen...  61.6 us
    reduce_scatter x1, waiting for transfers between devices, per_device(): lax.psum_scatter(w_key_grad.astype(jnp.bfloat16), 'fsdp', scatter_dimensi...  60.6 us
    all_gather x1, waiting for transfers between devices, gather_inward(): lax.all_gather(w_expand, 'fsdp', axis=0, tiled=True)  58.2 us
    all_gather x1, waiting for transfers between devices, per_device(): lax.all_gather(norm_two.astype(jnp.bfloat16), 'tp', axis=1, tiled=True)  53.7 us
    reduce_scatter x1, waiting for transfers between devices, per_device(): lax.psum_scatter(first_terms.astype(jnp.bfloat16), 'tp', scatter_dimensio...  50.8 us
  transfers between devices with their start and end apart: 20, of which 14 were waited for; matrix products, arithmetic and copies ran while one was open for 35% of the time, Pallas kernels for 0%

commit v1 on v0

--- a/solution.py
+++ b/solution.py
@@ -167,7 +167,16 @@
     ).astype(jnp.float32)
     middle = frames_wide + attn_part + out_bias
     norm_two, normed_two, inverse_two = layer_norm(middle, gain_two, shift_two)
-    second_rows = lax.all_gather(norm_two.astype(jnp.bfloat16), "tp", axis=1, tiled=True)
+    value = norm_two.astype(jnp.bfloat16)
+    ways, here = (lax.axis_size("tp"), lax.axis_index("tp"))
+    grown, reach = (value, 1)
+    while reach < ways:
+        theirs = lax.ppermute(grown, "tp", [(d, d ^ reach) for d in range(ways)])
+        mine_first = jnp.concatenate([grown, theirs], axis=1)
+        theirs_first = jnp.concatenate([theirs, grown], axis=1)
+        grown = jnp.where(here & reach == 0, mine_first, theirs_first)
+        reach = 2 * reach
+    second_rows = grown
     expanded = jnp.einsum(
         "csd,df->csf", second_rows, we_all, preferred_element_type=jnp.float32
     ) + be_all.astype(jnp.float32)

time: 1340 us -> 1290 us (0.963)
  waiting for transfers between devices: 571 us -> 509 us
    all_gather x1 -> x0, waiting for transfers between devices: 53.7 us -> none  [per_device(): lax.all_gather(norm_two.astype(jnp.bfloat16), 'tp', axis=1, tiled=True)]
  transfers between devices with their start and end apart: 20 -> 20, of which waited for: 14 -> 13; matrix products, arithmetic and copies ran while one was open for 35% -> 37% of each run, Pallas kernels for 0% -> 0%
where the time goes in v1:
time: 1290 us; the launch traced here: 1280 us
  waiting for transfers between devices  509 us (39%)
  matrix products  387 us (30%)
  blocking collectives  205 us (16%)
  other arithmetic  133 us (10%)
  local copies, waits for them, and re-layouts  28.3 us (2%)
  between operations  17.9 us (1%)
    unnamed x4, blocking collectives  205 us
    all_gather x1, waiting for transfers between devices, gather_outward(): lax.all_gather(w_reduce, 'fsdp', axis=1, tiled=True)  66 us
    convert_element_type x1, other arithmetic, attend_back(): score_grad = (probs * (weight_grad - row_inner)).astype(jnp.bfloat16)  62.3 us
    reduce_scatter x1, waiting for transfers between devices, per_device(): lax.psum_scatter(w_query_grad.astype(jnp.bfloat16), 'fsdp', scatter_dimen...  61.6 us
    reduce_scatter x1, waiting for transfers between devices, per_device(): lax.psum_scatter(w_key_grad.astype(jnp.bfloat16), 'fsdp', scatter_dimensi...  60.5 us
    all_gather x1, waiting for transfers between devices, gather_inward(): lax.all_gather(w_expand, 'fsdp', axis=0, tiled=True)  59.8 us
    reduce_scatter x1, waiting for transfers between devices, per_device(): lax.psum_scatter(first_terms.astype(jnp.bfloat16), 'tp', scatter_dimensio...  51 us
    dot_general x1, matrix products, attend_back(): jnp.einsum('qhe,khe->hqk', context_grad, value_rows, preferred_element_ty...  50.6 us
  transfers between devices with their start and end apart: 20, of which 13 were waited for; matrix products, arithmetic and copies ran while one was open for 37% of the time, Pallas kernels for 0%

profile of v1, /device:TPU:0, one launch (start us, length us, event | category | flops | bytes accessed | tf_op | source)
XLA Modules:
  0.0 1281.5 jit_solution(10887154242647106296)
XLA Ops:
  13.1 43.0 %all-reduce.19 = (bf16[1280]{0:T(1024)(128)(2,1)}, bf16[1280]{0:T(1024)(128)(2,1)}, bf16[1280]{0:T(1024)(128)(2,1)}, bf16[1280]{0:T(1024)(128)(2,1)S(1)}, bf16[1...) all-reduce(bf16[1280]{0:T(1024)(128)(2,1)S(1)} %dynamic-update-slice, ...), channel_id=1, replica_groups=mesh['fsdp'=16,'tp'=2] {'fsdp','tp'}, use_global_device_ids=true, to_apply=%add.6 | all-reduce | flops 7680 | bytes 30720
  56.1 1.9 convert_reduce_fusion.2
  58.0 2.2 fusion.35
  60.9 2.0 fusion.30
  70.1 60.1 %all-reduce.21 = (bf16[640]{0:T(1024)(128)(2,1)S(1)}, bf16[640]{0:T(1024)(128)(2,1)S(1)}, bf16[2560]{0:T(1024)(128)(2,1)}) all-reduce(bf16[640]{0:T(1024)(128)(2,1)S(1)} %dynamic-update-slice.2, bf16[640]{0:T(1024)(128)(2,1)S(1)} %dynamic-update-slice.3, ...), channel_id=1, replica_groups=mesh['fsdp'=16,'tp'=2] {'fsdp'}, use_global_device_ids=true, to_apply=%add.2 | all-reduce | flops 3840 | bytes 15360
  130.3 7.0 multiply_convert_fusion.2
  137.3 2.7 copy.57
  140.0 18.1 %all-gather.12.cloned.1.call-done = bf16[1280,640]{1,0:T(8,128)(2,1)} async-done(((bf16[80,640]{1,0:T(8,128)(2,1)}), bf16[1280,640]{1,0:T(8,128)(2,1)}) %all-gather.12.cloned.1.call-update) | async-done | bytes 1638416 | tf_op jit(solution)/shard_map/all_gather | solution.py:78
  158.1 7.0 add_convert_fusion.3
  165.1 4.0 copy.56
  169.1 29.9 %all-gather.16.cloned.1.call-done = bf16[1280,640]{1,0:T(8,128)(2,1)} async-done(((bf16[80,640]{1,0:T(8,128)(2,1)}), bf16[1280,640]{1,0:T(8,128)(2,1)}) %all-gather.16.cloned.1.call-update) | async-done | bytes 1638416 | tf_op jit(solution)/shard_map/all_gather | solution.py:77
  199.0 7.0 fusion.77
  206.0 4.0 copy.58
  210.0 28.8 %fusion.101 = (f32[8,1504]{1,0:T(8,128)S(1)}, f32[8,1504,1504]{1,2,0:T(8,128)}) fusion(bf16[1504,8,80]{0,2,1:T(8,128)(2,1)S(1)} %bitcast.112, bf16[1504,8,80]{0,2,1:T(8,128)(2,1)} %bitcast.114, pred[1504]{0:T(1024)(128)(4,1)S(1)} %iota_compare_fusion), kind=kOutput, calls=%fused_computation.139 | convolution fusion | flops 2931560704 | bytes 76284384 | tf_op jit(solution)/shard_map/while/body/eval_jaxpr/qhe,khe->hqk/dot_general | solution.py:34
  238.8 23.5 %fusion = f32[8,1504]{1,0:T(8,128)S(1)} fusion(f32[8,1504,1504]{1,2,0:T(8,128)} %get-tuple-element.104, f32[8,1504]{1,0:T(8,128)S(1)} %get-tuple-element.103), kind=kLoop, calls=%fused_computation.5 | loop fusion | flops 36180224 | bytes 72480768 | tf_op jit(solution)/shard_map/while/body/eval_jaxpr/reduce_sum | solution.py:44
  262.3 27.5 %fusion.92 = bf16[8,80,1504]{2,1,0:T(8,128)(2,1)} fusion(bf16[1504,8,80]{0,2,1:T(8,128)(2,1)S(1)} %bitcast.117, f32[8,1504,1504]{1,2,0:T(8,128)} %get-tuple-element.104, f32[8,1504]{1,0:T(8,128)S(1)} %fusion, f32[8,1504]{1,0:T(8,128)S(1)} %get-tuple-element.103), kind=kOutput, calls=%fused_computation.114 | convolution fusion | flops 2950631424 | bytes 76331008 | tf_op jit(solution)/shard_map/while/body/eval_jaxpr/hqk,khe->qhe/dot_general | solution.py:46
  289.8 7.1 fusion.17
  299.0 48.1 %reduce-scatter.11.cloned.1.call-done = bf16[1,752,1280]{2,1,0:T(8,128)(2,1)} async-done(((bf16[1,1504,1280]{2,1,0:T(8,128)(2,1)}), bf16[1,752,1280]{2,1,0:T(8,128)(2,1)}) %reduce-scatter.11.cloned.1.call-update) | async-done | bytes 1925136 | tf_op jit(solution)/shard_map/reduce_scatter | solution.py:165
  347.1 2.4 fusion.93
  350.5 2.4 add_convert_fusion.2
  353.3 59.8 %all-gather.20.cloned.1.call-done = bf16[1280,2560]{1,0:T(8,128)(2,1)} async-done(((bf16[80,2560]{1,0:T(8,128)(2,1)}), bf16[1280,2560]{1,0:T(8,128)(2,1)}) %all-gather.20.cloned.1.call-update) | async-done | bytes 6553616 | tf_op jit(solution)/shard_map/all_gather | solution.py:81
  413.1 50.3 %multiply_convert_fusion.1 = (bf16[1504,2560]{1,0:T(8,128)(2,1)}, f32[1504,2560]{1,0:T(8,128)}, f32[1504,2560]{1,0:T(8,128)}) fusion(f32[2560]{0:T(1024)S(1)} %convert_element_type.231, bf16[1280,2560]{1,0:T(8,128)(2,1)} %all-gather.20.cloned.1.call-done, bf16[752,1280]{1,0:T(8,128)(2,1)S(1)} %bitcast.124, bf16[752,1280]{1,0:T(8,128)(2,1)} %bitcast.8, ...), kind=kOutput, calls=%fused_computation.14 | convolution fusion | flops 10128056320 | bytes 48916480 | tf_op jit(solution)/shard_map/csd,df->csf/dot_general | solution.py:180
  463.4 2.7 all-gather.24.cloned.1.call-done
  466.1 66.0 %all-gather.22.cloned.1.call-done = bf16[2560,1280]{0,1:T(8,128)(2,1)} async-done(((bf16[2560,80]{0,1:T(8,128)(2,1)}), bf16[2560,1280]{0,1:T(8,128)(2,1)}) %all-gather.22.cloned.1.call-update) | async-done | bytes 6553616 | tf_op jit(solution)/shard_map/all_gather | solution.py:89
  532.1 27.7 %fusion.102 = (bf16[2560]{0:T(1024)(128)(2,1)}, bf16[1504,2560]{1,0:T(8,128)(2,1)}) fusion(f32[1504,2560]{1,0:T(8,128)} %get-tuple-element.98, bf16[2560,1280]{0,1:T(8,128)(2,1)} %all-gather.22.cloned.1.call-done, bf16[1,1504,1280]{2,1,0:T(8,128)(2,1)} %all-gather.24.cloned.1.call-done, f32[1504,2560]{1,0:T(8,128)} %get-tuple-element.105, ...), kind=kOutput, calls=%fused_computation.140 | convolution fusion | flops 9918216192 | bytes 48921600 | tf_op jit(solution)/shard_map/csd,fd->csf/dot_general | solution.py:200
  559.8 15.6 %fusion.16 = bf16[1,1504,1280]{2,1,0:T(8,128)(2,1)} fusion(bf16[1504,2560]{1,0:T(8,128)(2,1)} %get-tuple-element.113, bf16[1280,2560]{1,0:T(8,128)(2,1)} %all-gather.20.cloned.1.call-done), kind=kOutput, calls=%fused_computation.38 | convolution fusion | flops 9858539520 | bytes 18104320 | tf_op jit(solution)/shard_map/csf,df->csd/dot_general | solution.py:206
  575.5 15.6 %fusion.15 = bf16[1,1504,1280]{2,1,0:T(8,128)(2,1)} fusion(bf16[1504,2560]{1,0:T(8,128)(2,1)} %get-tuple-element.97, bf16[2560,1280]{0,1:T(8,128)(2,1)} %all-gather.22.cloned.1.call-done), kind=kOutput, calls=%fused_computation.37 | convolution fusion | flops 9858539520 | bytes 18104320 | tf_op jit(solution)/shard_map/csf,fd->csd/dot_general | solution.py:185
  591.8 33.4 %reduce-scatter.15.cloned.1.call-done = bf16[1,752,1280]{2,1,0:T(8,128)(2,1)} async-done(((bf16[1,1504,1280]{2,1,0:T(8,128)(2,1)}), bf16[1,752,1280]{2,1,0:T(8,128)(2,1)}) %reduce-scatter.15.cloned.1.call-update) | async-done | bytes 1925136 | tf_op jit(solution)/shard_map/reduce_scatter | solution.py:209
  625.2 5.0 fusion.41
  630.2 48.4 %reduce-scatter.13.cloned.1.call-done = bf16[1,752,1280]{2,1,0:T(8,128)(2,1)} async-done(((bf16[1,1504,1280]{2,1,0:T(8,128)(2,1)}), bf16[1,752,1280]{2,1,0:T(8,128)(2,1)}) %reduce-scatter.13.cloned.1.call-update) | async-done | bytes 1925136 | tf_op jit(solution)/shard_map/reduce_scatter | solution.py:188
  678.6 7.6 convert_reduce_fusion.5
  686.3 15.6 %convolution_convert_fusion = bf16[2560,1280]{0,1:T(8,128)(2,1)} fusion(bf16[1504,2560]{1,0:T(8,128)(2,1)} %get-tuple-element.97, bf16[1,1504,1280]{2,1,0:T(8,128)(2,1)} %all-gather.24.cloned.1.call-done), kind=kOutput, calls=%fused_computation.28 | convolution fusion | flops 9859891200 | bytes 18104320 | tf_op jit(solution)/shard_map/csf,csd->fd/dot_general | solution.py:199
  702.0 1.5 copy-done.44
  703.5 17.2 %convolution_convert_fusion.1 = bf16[1280,2560]{1,0:T(8,128)(2,1)} fusion(bf16[1504,2560]{1,0:T(8,128)(2,1)} %get-tuple-element.113, bf16[752,1280]{1,0:T(8,128)(2,1)S(1)} %bitcast.125, bf16[752,1280]{1,0:T(8,128)(2,1)} %bitcast.8, pred[]{:T(512)S(6)} %eq.25), kind=kOutput, calls=%fused_computation.29 | convolution fusion | flops 9877217280 | bytes 18104320 | tf_op jit(solution)/shard_map/csd,csf->df/dot_general | solution.py:203
  721.5 17.7 %all-gather.26.cloned.1.call-done = bf16[1,1504,1280]{2,1,0:T(8,128)(2,1)} async-done(((bf16[1,752,1280]{2,1,0:T(8,128)(2,1)}), bf16[1,1504,1280]{2,1,0:T(8,128)(2,1)}) %all-gather.26.cloned.1.call-update) | async-done | bytes 3850256 | tf_op jit(solution)/shard_map/all_gather | solution.py:218
  739.3 6.5 fusion.86
  745.8 2.7 copy.60
  748.5 7.4 fusion.89
  755.9 50.6 %multiply_reduce_fusion = (f32[8,1504]{1,0:T(8,128)S(1)}, f32[8,1504,1504]{1,2,0:T(8,128)}) fusion(f32[8,1504,1504]{1,2,0:T(8,128)} %get-tuple-element.104, f32[8,1504]{1,0:T(8,128)S(1)} %log_add_fusion, bf16[1504,8,80]{0,2,1:T(8,128)(2,1)S(1)} %bitcast.110, bf16[1504,8,80]{0,2,1:T(8,128)(2,1)} %bitcast.116), kind=kOutput, calls=%fused_computation.1 | convolution fusion | flops 2949656832 | bytes 148715520 | tf_op jit(solution)/shard_map/while/body/eval_jaxpr/qhe,khe->hqk/dot_general | solution.py:58
  806.5 27.6 %bitcast_reduce_fusion = (bf16[8,80]{1,0:T(8,128)(2,1)S(1)}, bf16[8,80,1504]{2,1,0:T(8,128)(2,1)}) fusion(bf16[1504,8,80]{0,2,1:T(8,128)(2,1)S(1)} %bitcast.111, f32[8,1504,1504]{1,2,0:T(8,128)} %get-tuple-element.104, f32[8,1504]{1,0:T(8,128)S(1)} %log_add_fusion), kind=kOutput, calls=%fused_computation.115 | convolution fusion | flops 2933497344 | bytes 76284160 | tf_op jit(solution)/shard_map/while/body/eval_jaxpr/hqk,qhe->khe/dot_general | solution.py:55
  834.0 7.3 fusion.83
  841.4 62.3 %multiply_convert_fusion = bf16[8,1504,1504]{1,2,0:T(8,128)(2,1)} fusion(f32[8,1504,1504]{1,2,0:T(8,128)} %get-tuple-element.107, f32[8,1504,1504]{1,2,0:T(8,128)} %get-tuple-element.104, f32[8,1504]{1,0:T(8,128)S(1)} %get-tuple-element.106, f32[8,1504]{1,0:T(8,128)S(1)} %log_add_fusion), kind=kLoop, calls=%fused_computation | loop fusion | flops 72384512 | bytes 181057536 | tf_op jit(solution)/shard_map/while/body/eval_jaxpr/convert_element_type | solution.py:62
  903.7 15.1 %convert_reduce_fusion.4 = (f32[8,80]{1,0:T(8,128)S(1)}, bf16[8,80,1504]{2,1,0:T(8,128)(2,1)S(1)}) fusion(bf16[1504,8,80]{0,2,1:T(8,128)(2,1)S(1)} %bitcast.115, bf16[8,1504,1504]{1,2,0:T(8,128)(2,1)} %multiply_convert_fusion), kind=kOutput, calls=%fused_computation.62 | convolution fusion | flops 2898267648 | bytes 40045056 | tf_op jit(solution)/shard_map/while/body/eval_jaxpr/hqk,khe->qhe/dot_general | solution.py:63
  918.7 1.3 copy-done.9
  920.0 6.7 fusion.74
  926.8 18.6 %convolution_convert_fusion.5 = bf16[8,80,1504]{2,1,0:T(8,128)(2,1)} fusion(bf16[1504,8,80]{0,2,1:T(8,128)(2,1)S(1)} %bitcast.113, bf16[8,1504,1504]{1,2,0:T(8,128)(2,1)} %multiply_convert_fusion), kind=kOutput, calls=%fused_computation.106 | convolution fusion | flops 2896343040 | bytes 40042496 | tf_op jit(solution)/shard_map/while/body/eval_jaxpr/hqk,qhe->khe/dot_general | solution.py:66
  945.4 7.4 fusion.80
  952.9 4.8 fusion.104
  957.8 3.2 fusion.103
  961.0 5.2 fusion.18
  967.7 2.0 convert_element_type.275
  969.7 2.0 convert_element_type.272
  971.9 61.7 %all-reduce.20 = (bf16[640]{0:T(1024)(128)(2,1)S(1)}, bf16[640]{0:T(1024)(128)(2,1)S(1)}, bf16[2560]{0:T(1024)(128)(2,1)S(1)}) all-reduce(bf16[640]{0:T(1024)(128)(2,1)S(1)} %convert_element_type.265, bf16[640]{0:T(1024)(128)(2,1)S(1)} %reduce_sum.213, ...), channel_id=9, replica_groups=mesh['fsdp'=16,'tp'=2] {'fsdp'}, use_global_device_ids=true, to_apply=%region_21.22.clone | all-reduce | flops 3840 | bytes 15360
  1035.4 1.6 convert_element_type.269
  1037.0 8.1 reduce-scatter.23.cloned.1.call-done
  1045.1 1.6 convert_element_type.262
  1046.7 61.6 %reduce-scatter.19.cloned.1.call-done = bf16[80,640]{1,0:T(8,128)(2,1)} async-done(((bf16[1280,640]{1,0:T(8,128)(2,1)}), bf16[80,640]{1,0:T(8,128)(2,1)}) %reduce-scatter.19.cloned.1.call-update) | async-done | bytes 102416 | tf_op jit(solution)/shard_map/reduce_scatter | solution.py:256
  1108.3 1.6 convert_element_type.258
  1109.9 60.5 %reduce-scatter.21.cloned.1.call-done = bf16[80,640]{1,0:T(8,128)(2,1)} async-done(((bf16[1280,640]{1,0:T(8,128)(2,1)}), bf16[80,640]{1,0:T(8,128)(2,1)}) %reduce-scatter.21.cloned.1.call-update) | async-done | bytes 102416 | tf_op jit(solution)/shard_map/reduce_scatter | solution.py:259
  1170.4 1.6 convert_element_type.260
  1172.0 51.0 %reduce-scatter.17.cloned.1.call-done = bf16[1,752,1280]{2,1,0:T(8,128)(2,1)} async-done(((bf16[1,1504,1280]{2,1,0:T(8,128)(2,1)}), bf16[1,752,1280]{2,1,0:T(8,128)(2,1)}) %reduce-scatter.17.cloned.1.call-update) | async-done | bytes 1925136 | tf_op jit(solution)/shard_map/reduce_scatter | solution.py:247
  1223.0 3.4 fusion.42
  1226.5 40.1 %all-reduce.18 = (f32[1280]{0:T(1024)S(1)}, f32[1280]{0:T(1024)S(1)}, f32[1280]{0:T(1024)S(1)}, f32[1280]{0:T(1024)S(1)}, f32[1280]{0:T(1024)S(1)}, /*index=5*/f32[1280]{0:T(1024)S(1)}) all-reduce(f32[1280]{0:T(1024)S(1)} %copy-done.32, f32[1280]{0:T(1024)S(1)} %copy-done.33, ...), channel_id=12, replica_groups=mesh['fsdp'=16,'tp'=2] {'fsdp','tp'}, use_global_device_ids=true, to_apply=%region_26.27.clone | all-reduce | flops 7680 | bytes 61440
  1270.1 4.3 fusion.34
  (200 shorter events, 23.2 us)
Async XLA Ops:
  7.2 53.7 %copy-start = (bf16[1,752,1280]{2,1,0:T(8,128)(2,1)S(1)}, bf16[1,752,1280]{2,1,0:T(8,128)(2,1)}, u32[]{:S(2)}) copy-start(bf16[1,752,1280]{2,1,0:T(8,128)(2,1)} %param.19) | copy-start | bytes 5775364
  7.2 123.0 %all-gather.14.cloned.1.call-start = ((), (), s32[]{:S(2)}) async-start(), calls=%async_computation.12 | async-start | bytes 1740800 | tf_op jit(solution)/shard_map/all_gather | solution.py:76
  7.9 122.3 %all-gather.10.cloned.1.call-start = ((), (), s32[]{:S(2)}) async-start(), calls=%async_computation.10 | async-start | bytes 5775360 | tf_op jit(solution)/shard_map/all_gather | solution.py:142
  56.1 4.2 copy-start.22
  57.9 2.3 copy-start.24
  58.0 6.9 copy-start.42
  58.0 8.8 copy-start.47
  58.0 9.4 copy-start.48
  58.0 11.4 copy-start.49
  58.0 11.6 copy-start.50
  58.0 11.8 copy-start.51
  62.9 95.2 %all-gather.12.cloned.1.call-start = ((), (), s32[]{:S(2)}) async-start(), calls=%async_computation.11 | async-start | bytes 1740800 | tf_op jit(solution)/shard_map/all_gather | solution.py:78
  63.6 135.3 %all-gather.16.cloned.1.call-start = ((), (), s32[]{:S(2)}) async-start(), calls=%async_computation.13 | async-start | bytes 1740800 | tf_op jit(solution)/shard_map/all_gather | solution.py:77
  64.2 225.6 %all-gather.18.cloned.1.call-start = ((), (), s32[]{:S(2)}) async-start(), calls=%async_computation.14 | async-start | bytes 1740800 | tf_op jit(solution)/shard_map/all_gather | solution.py:88
  64.8 282.3 %reduce-scatter.11.cloned.1.call-start = ((), (), s32[]{:S(2)}) async-start(), calls=%async_computation.15 | async-start | bytes 5775360 | tf_op jit(solution)/shard_map/reduce_scatter | solution.py:165
  140.0 70.0 %copy-start.5 = (bf16[1504,640]{0,1:T(8,128)(2,1)}, bf16[1504,640]{0,1:T(8,128)(2,1)S(1)}, u32[]{:S(2)}) copy-start(bf16[1504,640]{0,1:T(8,128)(2,1)S(1)} %copy.57) | copy-start | bytes 5775364
  238.8 23.5 %copy-start.14 = (f32[8,1504]{1,0:T(8,128)}, f32[8,1504]{1,0:T(8,128)S(1)}, u32[]{:S(2)}) copy-start(f32[8,1504]{1,0:T(8,128)S(1)} %get-tuple-element.103) | copy-start | bytes 144388
  238.8 23.5 %copy-start.8 = (bf16[1504,640]{0,1:T(8,128)(2,1)S(1)}, bf16[1504,640]{0,1:T(8,128)(2,1)}, u32[]{:S(2)}) copy-start(bf16[1504,640]{0,1:T(8,128)(2,1)} %copy.56) | copy-start | bytes 5775364
  262.3 27.5 %copy-start.18 = (f32[8,1504]{1,0:T(8,128)}, f32[8,1504]{1,0:T(8,128)S(1)}, u32[]{:S(2)}) copy-start(f32[8,1504]{1,0:T(8,128)S(1)} %fusion) | copy-start | bytes 144388
  296.9 2.0 copy-start.39
  296.9 50.2 %copy-start.1 = (bf16[1,752,1280]{2,1,0:T(8,128)(2,1)S(1)}, bf16[1,752,1280]{2,1,0:T(8,128)(2,1)}, u32[]{:S(2)}) copy-start(bf16[1,752,1280]{2,1,0:T(8,128)(2,1)} %param.19) | copy-start | bytes 5775364
  297.0 116.1 %all-gather.20.cloned.1.call-start = ((), (), s32[]{:S(2)}) async-start(), calls=%async_computation.16 | async-start | bytes 6963200 | tf_op jit(solution)/shard_map/all_gather | solution.py:81
  297.7 168.4 %all-gather.24.cloned.1.call-start = ((), (), s32[]{:S(2)}) async-start(), calls=%async_computation.19 | async-start | bytes 5775360 | tf_op jit(solution)/shard_map/all_gather | solution.py:198
  298.5 233.7 %all-gather.22.cloned.1.call-start = ((), (), s32[]{:S(2)}) async-start(), calls=%async_computation.17 | async-start | bytes 6963200 | tf_op jit(solution)/shard_map/all_gather | solution.py:89
  299.0 51.5 %copy-start.16 = (f32[1280]{0:T(1024)}, f32[1280]{0:T(1024)S(1)}, u32[]{:S(2)}) copy-start(f32[1280]{0:T(1024)S(1)} %convert_element_type.227) | copy-start | bytes 15364
  299.0 51.5 %copy-start.20 = (f32[1280]{0:T(1024)}, f32[1280]{0:T(1024)S(1)}, u32[]{:S(2)}) copy-start(f32[1280]{0:T(1024)S(1)} %convert_element_type.228) | copy-start | bytes 15364
  347.1 2.4 copy-start.4
  349.5 3.4 copy-start.26
  350.5 2.8 copy-start.37
  350.5 2.4 copy-start.30
  352.9 60.2 %collective-permute-start = (bf16[1,752,1280]{2,1,0:T(8,128)(2,1)}, bf16[1,752,1280]{2,1,0:T(8,128)(2,1)S(1)}, u32[]{:S(2)}, u32[]{:S(2)}) collective-permute-start(bf16[1,752,1280]{2,1,0:T(8,128)(2,1)} %add_convert_fusion.2), channel_id=1, source_target_pairs={{0,1},{1,0},{2,3},{3,2},{4,5},{5,4},{6,7},{7,6},{8,9},{9,8},{10,11... | collective-permute-start | bytes 5775368 | tf_op jit(solution)/shard_map/ppermute | solution.py:174
  353.2 272.0 %reduce-scatter.15.cloned.1.call-start = ((), (), s32[]{:S(2)}) async-start(), calls=%async_computation.20 | async-start | bytes 5775360 | tf_op jit(solution)/shard_map/reduce_scatter | solution.py:209
  413.1 50.3 %copy-start.43 = (bf16[1,752,1280]{2,1,0:T(8,128)(2,1)}, bf16[1,752,1280]{2,1,0:T(8,128)(2,1)S(1)}, u32[]{:S(2)}) copy-start(bf16[1,752,1280]{2,1,0:T(8,128)(2,1)S(1)} %collective-permute-done) | copy-start | bytes 5775364
  575.4 103.2 %reduce-scatter.13.cloned.1.call-start = ((), (), s32[]{:S(2)}) async-start(), calls=%async_computation.18 | async-start | bytes 5775360 | tf_op jit(solution)/shard_map/reduce_scatter | solution.py:188
  591.1 34.1 %copy-start.2 = (bf16[1,752,1280]{2,1,0:T(8,128)(2,1)S(1)}, bf16[1,752,1280]{2,1,0:T(8,128)(2,1)}, u32[]{:S(2)}) copy-start(bf16[1,752,1280]{2,1,0:T(8,128)(2,1)} %param.19) | copy-start | bytes 5775364
  591.1 34.1 %copy-start.17 = (f32[1280]{0:T(1024)S(1)}, f32[1280]{0:T(1024)}, u32[]{:S(2)}) copy-start(f32[1280]{0:T(1024)} %copy-done.16) | copy-start | bytes 15364
  591.1 34.1 %copy-start.21 = (f32[1280]{0:T(1024)S(1)}, f32[1280]{0:T(1024)}, u32[]{:S(2)}) copy-start(f32[1280]{0:T(1024)} %copy-done.20) | copy-start | bytes 15364
  591.1 34.1 %copy-start.27 = (f32[752]{0:T(1024)S(1)}, f32[752]{0:T(1024)}, u32[]{:S(2)}) copy-start(f32[752]{0:T(1024)} %copy-done.26) | copy-start | bytes 9028
  591.1 34.1 %copy-start.31 = (f32[752]{0:T(1024)S(1)}, f32[752]{0:T(1024)}, u32[]{:S(2)}) copy-start(f32[752]{0:T(1024)} %copy-done.30) | copy-start | bytes 9028
  591.2 148.1 %all-gather.26.cloned.1.call-start = ((), (), s32[]{:S(2)}) async-start(), calls=%async_computation.21 | async-start | bytes 5775360 | tf_op jit(solution)/shard_map/all_gather | solution.py:218
  686.3 281.5 %reduce-scatter.29.cloned.1.call-start = ((), (), s32[]{:S(2)}) async-start(), calls=%async_computation.28 | async-start | bytes 6963200 | tf_op jit(solution)/shard_map/reduce_scatter | solution.py:282
  702.0 267.7 %reduce-scatter.27.cloned.1.call-start = ((), (), s32[]{:S(2)}) async-start(), calls=%async_computation.27 | async-start | bytes 6963200 | tf_op jit(solution)/shard_map/reduce_scatter | solution.py:271
  720.7 18.6 %copy-start.46 = (bf16[640,1280]{0,1:T(8,128)(2,1)S(1)}, bf16[640,1280]{0,1:T(8,128)(2,1)}, u32[]{:S(2)}) copy-start(bf16[640,1280]{0,1:T(8,128)(2,1)} %all-gather.18.cloned.1.call-done) | copy-start | bytes 4915204
  720.7 314.7 %reduce-scatter.25.cloned.1.call-start = ((), (), s32[]{:S(2)}) async-start(), calls=%async_computation.26 | async-start | bytes 1740800 | tf_op jit(solution)/shard_map/reduce_scatter | solution.py:279
  755.9 289.2 %reduce-scatter.23.cloned.1.call-start = ((), (), s32[]{:S(2)}) async-start(), calls=%async_computation.25 | async-start | bytes 1740800 | tf_op jit(solution)/shard_map/reduce_scatter | solution.py:262
  841.3 267.0 %reduce-scatter.19.cloned.1.call-start = ((), (), s32[]{:S(2)}) async-start(), calls=%async_computation.23 | async-start | bytes 1740800 | tf_op jit(solution)/shard_map/reduce_scatter | solution.py:256
  841.4 62.3 %copy-start.7 = (bf16[1504,640]{0,1:T(8,128)(2,1)S(1)}, bf16[1504,640]{0,1:T(8,128)(2,1)}, u32[]{:S(2)}) copy-start(bf16[1504,640]{0,1:T(8,128)(2,1)} %copy.58) | copy-start | bytes 5775364
  920.0 6.8 copy-start.6
  926.8 243.6 %reduce-scatter.21.cloned.1.call-start = ((), (), s32[]{:S(2)}) async-start(), calls=%async_computation.24 | async-start | bytes 1740800 | tf_op jit(solution)/shard_map/reduce_scatter | solution.py:259
  945.4 7.4 copy-start.11
  952.8 270.2 %reduce-scatter.17.cloned.1.call-start = ((), (), s32[]{:S(2)}) async-start(), calls=%async_computation.22 | async-start | bytes 5775360 | tf_op jit(solution)/shard_map/reduce_scatter | solution.py:247
  952.9 4.9 copy-start.12
  952.9 4.9 copy-start.45
  957.7 3.3 copy-start.10
  957.8 3.3 copy-start.13
  966.2 5.6 copy-start.36
  966.2 256.8 %copy-start.3 = (bf16[1,752,1280]{2,1,0:T(8,128)(2,1)S(1)}, bf16[1,752,1280]{2,1,0:T(8,128)(2,1)}, u32[]{:S(2)}) copy-start(bf16[1,752,1280]{2,1,0:T(8,128)(2,1)} %param.19) | copy-start | bytes 5775364
  966.2 256.8 %copy-start.23 = (f32[1280]{0:T(1024)S(1)}, f32[1280]{0:T(1024)}, u32[]{:S(2)}) copy-start(f32[1280]{0:T(1024)} %copy-done.22) | copy-start | bytes 15364
  966.2 256.8 %copy-start.25 = (f32[752]{0:T(1024)S(1)}, f32[752]{0:T(1024)}, u32[]{:S(2)}) copy-start(f32[752]{0:T(1024)} %copy-done.24) | copy-start | bytes 9028
  966.2 256.8 %copy-start.29 = (f32[752]{0:T(1024)S(1)}, f32[752]{0:T(1024)}, u32[]{:S(2)}) copy-start(f32[752]{0:T(1024)} %copy-done.28) | copy-start | bytes 9028
  966.2 260.2 %copy-start.32 = (f32[1280]{0:T(1024)S(1)}, f32[1280]{0:T(1024)}, u32[]{:S(2)}) copy-start(f32[1280]{0:T(1024)} %get-tuple-element.94) | copy-start | bytes 15364
  966.3 260.2 %copy-start.33 = (f32[1280]{0:T(1024)S(1)}, f32[1280]{0:T(1024)}, u32[]{:S(2)}) copy-start(f32[1280]{0:T(1024)} %get-tuple-element.100) | copy-start | bytes 15364
  966.3 260.2 %copy-start.34 = (f32[1280]{0:T(1024)S(1)}, f32[1280]{0:T(1024)}, u32[]{:S(2)}) copy-start(f32[1280]{0:T(1024)} %get-tuple-element.68) | copy-start | bytes 15364
  966.3 260.2 %copy-start.35 = (f32[1280]{0:T(1024)S(1)}, f32[1280]{0:T(1024)}, u32[]{:S(2)}) copy-start(f32[1280]{0:T(1024)} %get-tuple-element.74) | copy-start | bytes 15364
  (8 other events, 9.7 us)
Sparse Core Ops, SparseCore 0:
  10.2 42.8 all-gather.13
  63.0 52.8 all-gather.9
  118.1 39.9 all-gather.11
  160.1 38.8 all-gather.15
  201.0 38.8 all-gather.17
  297.1 49.9 reduce-scatter.10
  349.6 63.3 all-gather.19
  414.7 51.4 all-gather.23
  468.7 63.3 all-gather.21
  575.6 49.6 reduce-scatter.14
  627.5 51.0 reduce-scatter.12
  686.4 52.8 all-gather.25
  743.7 86.9 reduce-scatter.28
  834.5 85.9 reduce-scatter.26
  924.5 58.3 reduce-scatter.24
  986.5 58.5 reduce-scatter.22
  1049.7 58.5 reduce-scatter.18
  1111.9 58.4 reduce-scatter.20
  1172.7 50.2 reduce-scatter.16
